TPU v7x, 32 devices: a whole 2x2x4 slice. The times are simulated.
32 devices in a mesh: dp: 16 (over z, y, core), tensor: 2 (over x).
Axes of the slice: x: 2, y: 2, z: 4, core: 2. Of those that a mesh axis runs over, the one named last changes fastest.
Arguments:
- tokens: bfloat16 [28672, 768], P(('dp', 'tensor')), may hold values from -6 to 6
- cotangent: bfloat16 [28672, 768], P(('dp', 'tensor')), may hold values from -6 to 6
- time_embed: float32 [16, 128], P('dp'), may hold values from -4 to 4
- block_parent: int32 [16, 14], P('dp'), may hold values from 0 to 5, as said below
- positions: int32 [28672], P('dp'), may hold values from 0 to 511, as said below
- gain_first: bfloat16 [768], P(('dp', 'tensor')), may hold values from 0.25 to 1.75
- inlet_weight: bfloat16 [768, 3, 12, 64], P('dp', None, 'tensor'), may hold values from -0.21875 to 0.21875
- outlet_weight: bfloat16 [12, 64, 768], P('tensor', None, 'dp'), may hold values from -0.875 to 0.875
- gain_second: bfloat16 [768], P(('dp', 'tensor')), may hold values from 0.25 to 1.75
- up_weight: bfloat16 [768, 3072], P(None, ('dp', 'tensor')), may hold values from -0.21875 to 0.21875
- up_bias: bfloat16 [3072], P(('dp', 'tensor')), may hold values from -3 to 3
- down_weight: bfloat16 [3072, 768], P(('dp', 'tensor')), may hold values from -0.109375 to 0.109375
- down_bias: bfloat16 [768], P(('dp', 'tensor')), may hold values from -2 to 2
- modulator: bfloat16 [128, 6, 768], P(None, None, ('dp', 'tensor')), may hold values from -0.5 to 0.5
- modulator_bias: bfloat16 [6, 768], P(None, ('dp', 'tensor')), may hold values from -3 to 3
Outputs:
- layer_output: bfloat16 [28672, 768], P(('dp', 'tensor'))
- adjoint_tokens: bfloat16 [28672, 768], P(('dp', 'tensor'))
- adjoint_gain_first: float32 [768], P(('dp', 'tensor'))
- adjoint_inlet: float32 [768, 3, 12, 64], P('dp', None, 'tensor')
- adjoint_outlet: float32 [12, 64, 768], P('tensor', None, 'dp')
- adjoint_gain_second: float32 [768], P(('dp', 'tensor'))
- adjoint_up_weight: float32 [768, 3072], P(None, ('dp', 'tensor'))
- adjoint_up_bias: float32 [3072], P(('dp', 'tensor'))
- adjoint_down_weight: float32 [3072, 768], P(('dp', 'tensor'))
- adjoint_down_bias: float32 [768], P(('dp', 'tensor'))
- adjoint_modulator: float32 [128, 6, 768], P(None, None, ('dp', 'tensor'))
- adjoint_modulator_bias: float32 [6, 768], P(None, ('dp', 'tensor'))
Inputs may be any that keep to these rules, and one draw needn't show every extreme that they name: block_parent[t, b] is the parent block of block b of tree t. Blocks 0 to 1 are the trunk: block 0 is its own parent and block b > 0 has parent b - 1. The next 4 blocks are branches, each with a trunk block as parent; the last 8 blocks are leaves, each with a branch block as parent. positions of a token = 128 times the number of strict ancestors of its block plus its place within its block.
All inputs are finite; a program needn't handle non-finite values.
Results may differ from a plain program's by a relative error of at most 0.02.
The roundings to bfloat16 on the way count: a program that leaves them out, or rounds other values in their place, can miss the bound.
Values may be sent and summed in bfloat16 or wider, within the bound.
No kernel may reach another device: no remote copies, remote signals or barrier semaphores. Data moves between devices by JAX's collectives and lax.ppermute only.
A program may use at most 192 MiB of HBM per device.

v0:
```python
from functools import partial
import jax
import jax.numpy as jnp
from jax import lax
from jax.sharding import PartitionSpec as P

EPS = 1e-05
ROPE_BASE = 10000.0
MASKED = -1e30
HIGHEST = lax.Precision.HIGHEST


def modulate(values, weight_gain, offset, stretch):
    center = values - jnp.mean(values, axis=-1, keepdims=True)
    second = jnp.mean(center * center, axis=-1, keepdims=True)
    return center * lax.rsqrt(second + EPS) * weight_gain * (1.0 + stretch) + offset


def rotary_tables(places, width):
    halfway = width // 2
    inverse = ROPE_BASE ** (-(jnp.arange(halfway, dtype=jnp.float32) * 2.0 / width))
    angles = places.astype(jnp.float32)[:, None] * inverse[None, :]
    return (jnp.cos(angles), jnp.sin(angles))


def rotate(vectors, cosine, sine_part):
    halfway = vectors.shape[-1] // 2
    former = vectors[..., :halfway]
    latter = vectors[..., halfway:]
    cosine = cosine[:, None, :]
    sine_part = sine_part[:, None, :]
    return jnp.concatenate(
        [former * cosine - latter * sine_part, latter * cosine + former * sine_part], axis=-1
    )


def path_mask(parents, length):
    amount = parents.shape[0]
    labels = jnp.arange(amount, dtype=jnp.int32)
    climb_map = (parents[:, None] == labels[None, :]).astype(jnp.float32)
    identity = jnp.eye(amount, dtype=jnp.float32)

    def climb(iteration, carried):
        reached, ancestry = carried
        reached = jnp.dot(reached, climb_map, precision=HIGHEST)
        return (reached, jnp.maximum(ancestry, reached))

    reached, ancestry = lax.fori_loop(0, amount, climb, (identity, identity))
    linked = jnp.maximum(ancestry, ancestry.T)
    owners = jnp.arange(length, dtype=jnp.int32) // (length // amount)
    chooser = (owners[:, None] == labels[None, :]).astype(jnp.float32)
    joined = jnp.dot(jnp.dot(chooser, linked, precision=HIGHEST), chooser.T, precision=HIGHEST)
    return joined > 0.5


def head_order(array):
    return jnp.transpose(array, (1, 0, 2))


def fetch_layer(inlet_weight, outlet_weight, up_weight, down_weight, up_bias):
    return (
        lax.all_gather(inlet_weight, "dp", axis=0, tiled=True),
        lax.all_gather(outlet_weight, "dp", axis=2, tiled=True),
        lax.all_gather(up_weight, "dp", axis=1, tiled=True),
        lax.all_gather(down_weight, "dp", axis=0, tiled=True),
        lax.all_gather(up_bias, "dp", axis=0, tiled=True),
    )


def head_forward(allowed, scale_factor, bundle):
    queries, keys_rot, values_v = bundle
    scores = jnp.dot(queries, keys_rot.T, preferred_element_type=jnp.float32)
    logits = jnp.where(allowed, scores * scale_factor, MASKED)
    highest = jnp.max(logits, axis=-1, keepdims=True)
    raised = jnp.exp(logits - highest)
    totals = jnp.sum(raised, axis=-1, keepdims=True)
    probs = raised / totals
    attended = jnp.dot(probs.astype(jnp.bfloat16), values_v, preferred_element_type=jnp.float32)
    return (attended.astype(jnp.bfloat16), (highest + jnp.log(totals))[:, 0])


def head_backward(allowed, scale_factor, bundle):
    queries, keys_rot, values_v, slope, log_total = bundle
    scores = jnp.dot(queries, keys_rot.T, preferred_element_type=jnp.float32)
    logits = jnp.where(allowed, scores * scale_factor, MASKED)
    probs = jnp.exp(logits - log_total[:, None])
    value_adj = jnp.dot(probs.astype(jnp.bfloat16).T, slope, preferred_element_type=jnp.float32)
    prob_slope = jnp.dot(slope, values_v.T, preferred_element_type=jnp.float32)
    inner = jnp.sum(probs * prob_slope, axis=-1, keepdims=True)
    score_slope = (probs * (prob_slope - inner) * scale_factor).astype(jnp.bfloat16)
    query_adj = jnp.dot(score_slope, keys_rot, preferred_element_type=jnp.float32)
    key_adj = jnp.dot(score_slope.T, queries, preferred_element_type=jnp.float32)
    return (query_adj, key_adj, value_adj)


def per_device(
    tokens,
    cotangent,
    time_embed,
    block_parent,
    positions,
    gain_first,
    inlet_weight,
    outlet_weight,
    gain_second,
    up_weight,
    up_bias,
    down_weight,
    down_bias,
    modulator,
    modulator_bias,
):
    smalls = (
        lax.all_gather(gain_first, ("dp", "tensor"), axis=0, tiled=True),
        lax.all_gather(gain_second, ("dp", "tensor"), axis=0, tiled=True),
        lax.all_gather(down_bias, ("dp", "tensor"), axis=0, tiled=True),
        lax.all_gather(modulator_bias, ("dp", "tensor"), axis=1, tiled=True),
        lax.all_gather(modulator, ("dp", "tensor"), axis=2, tiled=True),
    )
    norm_one, norm_two, bias_down, bias_mod, weight_mod = [
        member.astype(jnp.float32) for member in smalls
    ]
    width = tokens.shape[1]
    inlet_full, outlet_full, up_full, down_full, up_bias_full = fetch_layer(
        inlet_weight, outlet_weight, up_weight, down_weight, up_bias
    )
    local_heads = inlet_full.shape[2]
    head_width = inlet_full.shape[3]
    inlet_flat = inlet_full.reshape(width, -1)
    outlet_flat = outlet_full.reshape(local_heads * head_width, width)
    embed_act = jax.nn.silu(time_embed)
    shifts = (
        jnp.dot(embed_act, weight_mod.reshape(weight_mod.shape[0], -1), precision=HIGHEST).reshape(
            6, width
        )
        + bias_mod
    )
    values = tokens.astype(jnp.float32)
    normed = modulate(values, norm_one, shifts[0], shifts[1]).astype(jnp.bfloat16)
    normed_all = lax.all_gather(normed, "tensor", axis=0, tiled=True)
    length = normed_all.shape[0]
    mixed = jnp.dot(normed_all, inlet_flat, preferred_element_type=jnp.float32).reshape(
        length, 3, local_heads, head_width
    )
    cosine, sine_part = rotary_tables(positions, head_width)
    queries = head_order(rotate(mixed[:, 0], cosine, sine_part).astype(jnp.bfloat16))
    keys_rot = head_order(rotate(mixed[:, 1], cosine, sine_part).astype(jnp.bfloat16))
    values_v = head_order(mixed[:, 2].astype(jnp.bfloat16))
    allowed = path_mask(block_parent[0], length)
    scale_factor = head_width ** (-0.5)
    attended_heads, log_totals = lax.map(
        partial(head_forward, allowed, scale_factor), (queries, keys_rot, values_v)
    )
    attended = head_order(attended_heads).reshape(length, local_heads * head_width)
    branch_part = jnp.dot(attended, outlet_flat, preferred_element_type=jnp.float32)
    branch = lax.psum_scatter(
        branch_part.astype(jnp.bfloat16), "tensor", scatter_dimension=0, tiled=True
    ).astype(jnp.float32)
    middle = values + shifts[2] * branch
    normed_two = modulate(middle, norm_two, shifts[3], shifts[4]).astype(jnp.bfloat16)
    normed_two_all = lax.all_gather(normed_two, "tensor", axis=0, tiled=True)
    hidden = jnp.dot(
        normed_two_all, up_full, preferred_element_type=jnp.float32
    ) + up_bias_full.astype(jnp.float32)
    activated = jax.nn.gelu(hidden, approximate=True).astype(jnp.bfloat16)
    mlp_part = jnp.dot(activated, down_full, preferred_element_type=jnp.float32)
    mlp_out = lax.psum_scatter(
        mlp_part.astype(jnp.bfloat16), "tensor", scatter_dimension=0, tiled=True
    ).astype(jnp.float32)
    layer_output = (middle + shifts[5] * (mlp_out + bias_down)).astype(jnp.bfloat16)
    inlet_full, outlet_full, up_full, down_full, up_bias_full = fetch_layer(
        inlet_weight, outlet_weight, up_weight, down_weight, up_bias
    )
    inlet_flat = inlet_full.reshape(width, -1)
    outlet_flat = outlet_full.reshape(local_heads * head_width, width)
    slope = cotangent.astype(jnp.float32)
    gate_two_adj = jnp.sum(slope * (mlp_out + bias_down), axis=0)
    down_bias_adj = jnp.sum(slope, axis=0) * shifts[5]
    mlp_slope = (slope * shifts[5]).astype(jnp.bfloat16)
    mlp_slope_all = lax.all_gather(mlp_slope, "tensor", axis=0, tiled=True)
    down_adj = jnp.dot(activated.T, mlp_slope_all, preferred_element_type=jnp.float32)
    act_slope = jnp.dot(mlp_slope_all, down_full.T, preferred_element_type=jnp.float32)
    gelu_back = jax.vjp(partial(jax.nn.gelu, approximate=True), hidden)[1]
    hidden_slope = gelu_back(act_slope)[0].astype(jnp.bfloat16)
    up_bias_adj = jnp.sum(hidden_slope.astype(jnp.float32), axis=0)
    up_adj = jnp.dot(normed_two_all.T, hidden_slope, preferred_element_type=jnp.float32)
    norm_two_part = jnp.dot(hidden_slope, up_full.T, preferred_element_type=jnp.float32)
    norm_two_slope = lax.psum_scatter(
        norm_two_part.astype(jnp.bfloat16), "tensor", scatter_dimension=0, tiled=True
    ).astype(jnp.float32)
    middle_back = jax.vjp(modulate, middle, norm_two, shifts[3], shifts[4])[1]
    middle_adj, gain_two_adj, shift_two_adj, scale_two_adj = middle_back(norm_two_slope)
    middle_slope = slope + middle_adj
    gate_one_adj = jnp.sum(middle_slope * branch, axis=0)
    branch_slope = (middle_slope * shifts[2]).astype(jnp.bfloat16)
    branch_slope_all = lax.all_gather(branch_slope, "tensor", axis=0, tiled=True)
    outlet_adj = jnp.dot(attended.T, branch_slope_all, preferred_element_type=jnp.float32)
    attended_slope = jnp.dot(
        branch_slope_all, outlet_flat.T, preferred_element_type=jnp.float32
    ).astype(jnp.bfloat16)
    attended_slope = head_order(attended_slope.reshape(length, local_heads, head_width))
    query_adj, key_adj, value_adj = lax.map(
        partial(head_backward, allowed, scale_factor),
        (queries, keys_rot, values_v, attended_slope, log_totals),
    )
    query_adj = rotate(head_order(query_adj), cosine, -sine_part)
    key_adj = rotate(head_order(key_adj), cosine, -sine_part)
    mixed_slope = (
        jnp.stack([query_adj, key_adj, head_order(value_adj)], axis=1)
        .astype(jnp.bfloat16)
        .reshape(length, -1)
    )
    inlet_adj = jnp.dot(normed_all.T, mixed_slope, preferred_element_type=jnp.float32).reshape(
        width, 3, local_heads, head_width
    )
    normed_part = jnp.dot(mixed_slope, inlet_flat.T, preferred_element_type=jnp.float32)
    normed_slope = lax.psum_scatter(
        normed_part.astype(jnp.bfloat16), "tensor", scatter_dimension=0, tiled=True
    ).astype(jnp.float32)
    values_back = jax.vjp(modulate, values, norm_one, shifts[0], shifts[1])[1]
    values_adj, gain_one_adj, shift_one_adj, scale_one_adj = values_back(normed_slope)
    adjoint_tokens = (middle_slope + values_adj).astype(jnp.bfloat16)
    shift_adj = jnp.stack(
        [shift_one_adj, scale_one_adj, gate_one_adj, shift_two_adj, scale_two_adj, gate_two_adj]
    )
    mod_weight_adj = embed_act[0][:, None, None] * shift_adj[None]
    outlet_adj = outlet_adj.reshape(local_heads, head_width, width)
    inlet_share, outlet_share, up_share, down_share, up_bias_share = (
        lax.psum_scatter(inlet_adj, "dp", scatter_dimension=0, tiled=True),
        lax.psum_scatter(outlet_adj, "dp", scatter_dimension=2, tiled=True),
        lax.psum_scatter(up_adj, "dp", scatter_dimension=1, tiled=True),
        lax.psum_scatter(down_adj, "dp", scatter_dimension=0, tiled=True),
        lax.psum_scatter(up_bias_adj, "dp", scatter_dimension=0, tiled=True),
    )
    gain_one_share, gain_two_share, down_bias_share, mod_bias_share, mod_weight_share = (
        lax.psum_scatter(gain_one_adj, ("dp", "tensor"), scatter_dimension=0, tiled=True),
        lax.psum_scatter(gain_two_adj, ("dp", "tensor"), scatter_dimension=0, tiled=True),
        lax.psum_scatter(down_bias_adj, ("dp", "tensor"), scatter_dimension=0, tiled=True),
        lax.psum_scatter(shift_adj, ("dp", "tensor"), scatter_dimension=1, tiled=True),
        lax.psum_scatter(mod_weight_adj, ("dp", "tensor"), scatter_dimension=2, tiled=True),
    )
    return (
        layer_output,
        adjoint_tokens,
        gain_one_share,
        inlet_share,
        outlet_share,
        gain_two_share,
        up_share,
        up_bias_share,
        down_share,
        down_bias_share,
        mod_weight_share,
        mod_bias_share,
    )


def solution(mesh):
    in_specs = (
        P(("dp", "tensor"), None),
        P(("dp", "tensor"), None),
        P("dp", None),
        P("dp", None),
        P("dp"),
        P(("dp", "tensor")),
        P("dp", None, "tensor", None),
        P("tensor", None, "dp"),
        P(("dp", "tensor")),
        P(None, ("dp", "tensor")),
        P(("dp", "tensor")),
        P(("dp", "tensor"), None),
        P(("dp", "tensor")),
        P(None, None, ("dp", "tensor")),
        P(None, ("dp", "tensor")),
    )
    out_specs = (
        P(("dp", "tensor"), None),
        P(("dp", "tensor"), None),
        P(("dp", "tensor")),
        P("dp", None, "tensor", None),
        P("tensor", None, "dp"),
        P(("dp", "tensor")),
        P(None, ("dp", "tensor")),
        P(("dp", "tensor")),
        P(("dp", "tensor"), None),
        P(("dp", "tensor")),
        P(None, None, ("dp", "tensor")),
        P(None, ("dp", "tensor")),
    )
    return jax.shard_map(
        per_device, mesh=mesh, in_specs=in_specs, out_specs=out_specs, check_vma=False
    )
```

profile of v0, /device:TPU:0, one launch (start us, length us, event | category | flops | bytes accessed | tf_op | source)
XLA Modules:
  0.0 1269.2 jit_solution(4032610746774366570)
XLA Ops:
  11.3 42.1 %all-reduce.10 = (bf16[768]{0:T(1024)(128)(2,1)}, bf16[768]{0:T(1024)(128)(2,1)S(1)}, bf16[768]{0:T(1024)(128)(2,1)}) all-reduce(bf16[768]{0:T(1024)(128)(2,1)S(1)} %dynamic-update-slice.1, bf16[768]{0:T(1024)(128)(2,1)S(1)} %dynamic-update-slice, ...), channel_id=1, replica_groups=mesh['dp'=16,'tensor'=2] {'dp','tensor'}, use_global_device_ids=true, to_apply=%add.1 | all-reduce | flops 2304 | bytes 9216
  53.4 67.6 %all-gather = bf16[32,24,6]{1,2,0:T(8,128)(2,1)S(1)} all-gather(bf16[1,24,6]{1,2,0:T(8,128)(2,1)} %bitcast.206), channel_id=1, replica_groups=mesh['dp'=16,'tensor'=2] {'dp','tensor'}, dimensions={0}, use_global_device_ids=true | all-gather | bytes 9504 | tf_op jit(solution)/shard_map/all_gather | solution.py:117
  143.4 22.4 %all_gather.51 = bf16[6,64,768]{1,2,0:T(8,128)(2,1)} all-gather(bf16[6,64,48]{1,2,0:T(8,128)(2,1)S(1)} %copy-done.23), channel_id=1, replica_groups=mesh['dp'=16,'tensor'=2] {'dp'}, dimensions={2}, use_global_device_ids=true | all-gather | bytes 626688 | tf_op jit(solution)/shard_map/all_gather | solution.py:63
  194.6 59.2 %while.39 = (s32[]{:T(128)}, bf16[6,1792,64]{1,2,0:T(8,128)(2,1)}, f32[6,1792]{1,0:T(8,128)S(1)}, bf16[6,1792,64]{2,1,0:T(8,128)(2,1)}, bf16[6,1792,64]{2,1,0:T(...) while((s32[]{:T(128)}, bf16[6,1792,64]{1,2,0:T(8,128)(2,1)}, ...), condition=%wide.region_7.8_spmd, body=%wide.region_4.7_spmd.sunk | while | flops 847886592 | bytes 43440232 | solution.py:151
  260.6 35.3 %reduce-scatter.11.cloned.1.call-done = bf16[896,768]{1,0:T(8,128)(2,1)} async-done(((bf16[1792,768]{1,0:T(8,128)(2,1)}), bf16[896,768]{1,0:T(8,128)(2,1)}) %reduce-scatter.11.cloned.1.call-update) | async-done | bytes 1376272 | tf_op jit(solution)/shard_map/reduce_scatter | solution.py:156
  306.4 33.3 %all-reduce.2 = bf16[1536]{0:T(1024)(128)(2,1)S(1)} all-reduce(bf16[1536]{0:T(1024)(128)(2,1)S(1)} %dynamic-update-slice.2), channel_id=1, replica_groups=mesh['dp'=16,'tensor'=2] {'dp'}, use_global_device_ids=true, to_apply=%add.2 | all-reduce | flops 1536 | bytes 6144
  340.6 41.2 %all-gather.16.cloned.1.call-done = bf16[1792,768]{1,0:T(8,128)(2,1)} async-done(((bf16[896,768]{1,0:T(8,128)(2,1)}), bf16[1792,768]{1,0:T(8,128)(2,1)}) %all-gather.16.cloned.1.call-update) | async-done | bytes 2752528 | tf_op jit(solution)/shard_map/all_gather | solution.py:161
  381.7 12.3 multiply_convert_fusion.1
  394.0 32.4 %all-gather.20.cloned.1.call-done = bf16[1536,768]{1,0:T(8,128)(2,1)} async-done(((bf16[96,768]{1,0:T(8,128)(2,1)}), bf16[1536,768]{1,0:T(8,128)(2,1)}) %all-gather.20.cloned.1.call-update) | async-done | bytes 2359312 | tf_op jit(solution)/shard_map/all_gather | solution.py:65
  426.4 40.8 %all-gather.22.cloned.1.call-done = bf16[1792,768]{1,0:T(8,128)(2,1)} async-done(((bf16[896,768]{1,0:T(8,128)(2,1)}), bf16[1792,768]{1,0:T(8,128)(2,1)}) %all-gather.22.cloned.1.call-update) | async-done | bytes 2752528 | tf_op jit(solution)/shard_map/all_gather | solution.py:180
  467.1 15.4 %convert_reduce_fusion = (f32[1536]{0:T(1024)}, bf16[1792,1536]{1,0:T(8,128)(2,1)S(1)}) fusion(f32[1792,1536]{1,0:T(8,128)} %get-tuple-element.307, f32[1536]{0:T(1024)S(1)} %convert_element_type.125, bf16[1792,768]{1,0:T(8,128)(2,1)} %all-gather.22.cloned.1.call-done, bf16[1536,768]{1,0:T(8,128)(2,1)} %all-gather.20.cloned.1.call-done), kind=kOutput, calls=%fused_computation.63 | convolution fusion | flops 4291164672 | bytes 21639168 | tf_op jit(solution)/shard_map/dot_general | solution.py:182
  500.8 29.1 %reduce-scatter.15.cloned.1.call-done = bf16[896,768]{1,0:T(8,128)(2,1)} async-done(((bf16[1792,768]{1,0:T(8,128)(2,1)}), bf16[896,768]{1,0:T(8,128)(2,1)}) %reduce-scatter.15.cloned.1.call-update) | async-done | bytes 1376272 | tf_op jit(solution)/shard_map/reduce_scatter | solution.py:188
  535.9 35.1 %reduce-scatter.13.cloned.1.call-done = bf16[896,768]{1,0:T(8,128)(2,1)} async-done(((bf16[1792,768]{1,0:T(8,128)(2,1)}), bf16[896,768]{1,0:T(8,128)(2,1)}) %reduce-scatter.13.cloned.1.call-update) | async-done | bytes 1376272 | tf_op jit(solution)/shard_map/reduce_scatter | solution.py:167
  582.6 38.1 %all-gather.24.cloned.1.call-done = bf16[1792,768]{1,0:T(8,128)(2,1)} async-done(((bf16[896,768]{1,0:T(8,128)(2,1)}), bf16[1792,768]{1,0:T(8,128)(2,1)}) %all-gather.24.cloned.1.call-update) | async-done | bytes 2752528 | tf_op jit(solution)/shard_map/all_gather | solution.py:196
  628.9 154.9 %while.40 = (s32[]{:T(128)}, f32[6,1792,64]{1,2,0:T(8,128)}, f32[6,1792,64]{1,2,0:T(8,128)}, bf16[6,1792,64]{1,2,0:T(8,128)(2,1)}, bf16[6,1792,64]{2,1,0:T(8,128...) while((s32[]{:T(128)}, f32[6,1792,64]{1,2,0:T(8,128)}, ...), condition=%wide.region_17.18_spmd, body=%wide.region_15.17_spmd.sunk | while | flops 2087319808 | bytes 155558096 | solution.py:202
  798.2 10.0 fusion.114
  808.4 10.1 fusion.115
  824.8 10.4 fusion.55
  844.1 33.7 %all-reduce.6 = f32[1536]{0:T(1024)S(1)} all-reduce(f32[1536]{0:T(1024)S(1)} %copy-done.38), channel_id=11, replica_groups=mesh['dp'=16,'tensor'=2] {'dp'}, use_global_device_ids=true, to_apply=%region_29.30.clone | all-reduce | flops 1536 | bytes 12288
  878.5 39.2 %all-reduce.9 = (f32[768]{0:T(1024)S(1)}, f32[768]{0:T(1024)S(1)}, f32[768]{0:T(1024)S(1)}, f32[6,768]{1,0:T(8,128)S(1)}) all-reduce(f32[768]{0:T(1024)S(1)} %get-tuple-element.216, f32[768]{0:T(1024)S(1)} %copy-done.33, f32[768]{0:T(1024)S(1)} %mul.488, ...), channel_id=6, replica_groups=mesh['dp'=16,'tensor'=2] {'dp','tensor'}, use_global_device_ids=true, to_apply=%region_22.23.clone | all-reduce | flops 6912 | bytes 55296
  923.6 73.9 %reduce-scatter.25.cloned.1.call-done = f32[96,768]{1,0:T(8,128)} async-done(((f32[1536,768]{1,0:T(8,128)}), f32[96,768]{1,0:T(8,128)}) %reduce-scatter.25.cloned.1.call-update) | async-done | bytes 294928 | tf_op jit(solution)/shard_map/reduce_scatter | solution.py:232
  997.5 66.6 %reduce-scatter.21.cloned.1.call-done = f32[6,64,48]{1,2,0:T(8,128)} async-done(((f32[6,64,768]{1,2,0:T(8,128)}), f32[6,64,48]{1,2,0:T(8,128)}) %reduce-scatter.21.cloned.1.call-update) | async-done | bytes 73744 | tf_op jit(solution)/shard_map/reduce_scatter | solution.py:230
  1064.1 93.3 %reduce-scatter.19.cloned.1.call-done = f32[48,3,6,64]{3,0,2,1:T(8,128)} async-done(((f32[768,3,6,64]{3,0,2,1:T(8,128)}), f32[48,3,6,64]{3,0,2,1:T(8,128)}) %reduce-scatter.19.cloned.1.call-update) | async-done | bytes 221200 | tf_op jit(solution)/shard_map/reduce_scatter | solution.py:229
  1157.5 105.0 %reduce-scatter.27.cloned.1.call-done = f32[128,6,24]{0,2,1:T(8,128)} async-done(((f32[128,6,768]{0,2,1:T(8,128)}), f32[128,6,24]{0,2,1:T(8,128)}) %reduce-scatter.27.cloned.1.call-update) | async-done | bytes 73744 | tf_op jit(solution)/shard_map/reduce_scatter | solution.py:240
  (366 shorter events, 368.2 us)
Async XLA Ops:
  7.2 115.8 %copy-start.3 = (bf16[896,768]{1,0:T(8,128)(2,1)S(1)}, bf16[896,768]{1,0:T(8,128)(2,1)}, u32[]{:S(2)}) copy-start(bf16[896,768]{1,0:T(8,128)(2,1)} %param.21) | copy-start | bytes 4128772
  7.2 116.4 %copy-start.42 = (f32[1,128]{1,0:T(1,128)S(1)}, f32[1,128]{1,0:T(1,128)}, u32[]{:S(2)}) copy-start(f32[1,128]{1,0:T(1,128)} %param.23) | copy-start | bytes 1540
  7.2 116.4 %all-gather.10.cloned.1.call-start = ((), (), s32[]{:S(2)}) async-start(), calls=%async_computation.9 | async-start | bytes 1216512 | tf_op jit(solution)/shard_map/all_gather | solution.py:118
  7.9 159.6 %all-gather.14.cloned.1.call-start = ((), (), s32[]{:S(2)}) async-start(), calls=%async_computation.11 | async-start | bytes 3760128 | tf_op jit(solution)/shard_map/all_gather | solution.py:62
  8.7 163.6 %all-gather.12.cloned.1.call-start = ((), (), s32[]{:S(2)}) async-start(), calls=%async_computation.10 | async-start | bytes 4128768 | tf_op jit(solution)/shard_map/all_gather | solution.py:140
  53.4 74.9 %copy-start.18 = (f32[768]{0:T(1024)}, f32[768]{0:T(1024)S(1)}, u32[]{:S(2)}) copy-start(f32[768]{0:T(1024)S(1)} %convert_element_type.115) | copy-start | bytes 9220
  128.3 167.6 %reduce-scatter.11.cloned.1.call-start = ((), (), s32[]{:S(2)}) async-start(), calls=%async_computation.12 | async-start | bytes 4128768 | tf_op jit(solution)/shard_map/reduce_scatter | solution.py:156
  259.5 36.4 %copy-start.15 = (f32[768]{0:T(1024)S(1)}, f32[768]{0:T(1024)}, u32[]{:S(2)}) copy-start(f32[768]{0:T(1024)} %get-tuple-element.226) | copy-start | bytes 9220
  259.5 81.0 %all-gather.18.cloned.1.call-start = ((), (), s32[]{:S(2)}) async-start(), calls=%async_computation.14 | async-start | bytes 2506752 | tf_op jit(solution)/shard_map/all_gather | solution.py:64
  260.1 121.6 %all-gather.16.cloned.1.call-start = ((), (), s32[]{:S(2)}) async-start(), calls=%async_computation.13 | async-start | bytes 4128768 | tf_op jit(solution)/shard_map/all_gather | solution.py:161
  301.3 125.0 %all-gather.20.cloned.1.call-start = ((), (), s32[]{:S(2)}) async-start(), calls=%async_computation.15 | async-start | bytes 2506752 | tf_op jit(solution)/shard_map/all_gather | solution.py:65
  302.1 165.1 %all-gather.22.cloned.1.call-start = ((), (), s32[]{:S(2)}) async-start(), calls=%async_computation.17 | async-start | bytes 4128768 | tf_op jit(solution)/shard_map/all_gather | solution.py:180
  304.8 225.0 %reduce-scatter.15.cloned.1.call-start = ((), (), s32[]{:S(2)}) async-start(), calls=%async_computation.18 | async-start | bytes 4128768 | tf_op jit(solution)/shard_map/reduce_scatter | solution.py:188
  490.6 80.5 %reduce-scatter.13.cloned.1.call-start = ((), (), s32[]{:S(2)}) async-start(), calls=%async_computation.16 | async-start | bytes 4128768 | tf_op jit(solution)/shard_map/reduce_scatter | solution.py:167
  500.1 120.6 %all-gather.24.cloned.1.call-start = ((), (), s32[]{:S(2)}) async-start(), calls=%async_computation.19 | async-start | bytes 4128768 | tf_op jit(solution)/shard_map/all_gather | solution.py:196
  580.1 257.4 %reduce-scatter.17.cloned.1.call-start = ((), (), s32[]{:S(2)}) async-start(), calls=%async_computation.20 | async-start | bytes 4128768 | tf_op jit(solution)/shard_map/reduce_scatter | solution.py:217
  798.2 125.4 %reduce-scatter.23.cloned.1.call-start = ((), (), s32[]{:S(2)}) async-start(), calls=%async_computation.23 | async-start | bytes 5013504 | tf_op jit(solution)/shard_map/reduce_scatter | solution.py:231
  808.3 189.2 %reduce-scatter.25.cloned.1.call-start = ((), (), s32[]{:S(2)}) async-start(), calls=%async_computation.24 | async-start | bytes 5013504 | tf_op jit(solution)/shard_map/reduce_scatter | solution.py:232
  818.5 245.7 %reduce-scatter.21.cloned.1.call-start = ((), (), s32[]{:S(2)}) async-start(), calls=%async_computation.22 | async-start | bytes 2506752 | tf_op jit(solution)/shard_map/reduce_scatter | solution.py:230
  824.7 332.8 %reduce-scatter.19.cloned.1.call-start = ((), (), s32[]{:S(2)}) async-start(), calls=%async_computation.21 | async-start | bytes 7520256 | tf_op jit(solution)/shard_map/reduce_scatter | solution.py:229
  835.3 427.2 %reduce-scatter.27.cloned.1.call-start = ((), (), s32[]{:S(2)}) async-start(), calls=%async_computation.25 | async-start | bytes 2433024 | tf_op jit(solution)/shard_map/reduce_scatter | solution.py:240
  841.5 36.9 %copy-start.25 = (f32[768]{0:T(1024)S(1)}, f32[768]{0:T(1024)}, u32[]{:S(2)}) copy-start(f32[768]{0:T(1024)} %get-tuple-element.221) | copy-start | bytes 9220
  841.6 36.9 %copy-start.30 = (f32[768]{0:T(1024)S(1)}, f32[768]{0:T(1024)}, u32[]{:S(2)}) copy-start(f32[768]{0:T(1024)} %get-tuple-element.295) | copy-start | bytes 9220
  841.6 36.9 %copy-start.33 = (f32[768]{0:T(1024)S(1)}, f32[768]{0:T(1024)}, u32[]{:S(2)}) copy-start(f32[768]{0:T(1024)} %get-tuple-element.213) | copy-start | bytes 9220
  (57 other events, 191.3 us)
Sparse Core Ops, SparseCore 0:
  10.9 54.4 all-gather.9
  67.6 47.3 all-gather.13
  128.4 36.3 all-gather.11
  259.6 36.2 reduce-scatter.10
  298.1 42.4 all-gather.17
  342.5 39.1 all-gather.15
  384.0 42.3 all-gather.19
  427.9 39.1 all-gather.21
  490.7 39.0 reduce-scatter.14
  531.9 39.0 reduce-scatter.12
  580.2 40.4 all-gather.23
  798.3 39.0 reduce-scatter.16
  841.9 76.5 reduce-scatter.22
  922.7 74.7 reduce-scatter.24
  1001.7 62.4 reduce-scatter.20
  1068.6 88.8 reduce-scatter.18
  1163.2 99.2 reduce-scatter.26
where the time goes:
time: 1270 us
  waiting for transfers between devices  596 us (47%)
  matrix products  285 us (22%)
  blocking collectives  238 us (19%)
  other arithmetic  77.1 us (6%)
  local copies, waits for them, and re-layouts  54.1 us (4%)
  between operations  16.2 us (1%)
    unnamed x4, blocking collectives  148 us
    reduce_scatter x1, waiting for transfers between devices, per_device(): lax.psum_scatter(mod_weight_adj, ('dp', 'tensor'), scatter_dimension=2, t...  105 us
    reduce_scatter x1, waiting for transfers between devices, per_device(): lax.psum_scatter(inlet_adj, 'dp', scatter_dimension=0, tiled=True)  93.3 us
    reduce_scatter x1, waiting for transfers between devices, per_device(): lax.psum_scatter(down_adj, 'dp', scatter_dimension=0, tiled=True)  73.9 us
    all_gather x1, blocking collectives, per_device(): lax.all_gather(modulator_bias, ('dp', 'tensor'), axis=1, tiled=True)  67.6 us
    reduce_scatter x1, waiting for transfers between devices, per_device(): lax.psum_scatter(outlet_adj, 'dp', scatter_dimension=2, tiled=True)  66.6 us
    all_gather x1, waiting for transfers between devices, per_device(): normed_two_all = lax.all_gather(normed_two, 'tensor', axis=0, tiled=True)  41.2 us
    all_gather x1, waiting for transfers between devices, per_device(): mlp_slope_all = lax.all_gather(mlp_slope, 'tensor', axis=0, tiled=True)  40.8 us
  transfers between devices with their start and end apart: 17, of which 13 were waited for; matrix products, arithmetic and copies ran while one was open for 9% of the time, Pallas kernels for 0%

commit v1 on v0

--- a/solution.py
+++ b/solution.py
@@ -8,6 +8,26 @@
 ROPE_BASE = 10000.0
 MASKED = -1e30
 HIGHEST = lax.Precision.HIGHEST
+
+
+def column_order(raw, d0):
+    raw = jnp.moveaxis(raw, 0, d0)
+    part_next = raw.shape
+    return raw.reshape(*part_next[:d0], part_next[d0] * part_next[d0 + 1], *part_next[d0 + 2 :])
+
+
+def refer_the_pairs_all(work_x, axis_key):
+    n_axis = lax.axis_size(axis_key)
+    block_now = work_x[None]
+    for u in range(n_axis.bit_length() - 1):
+        odd = 1 << u
+        block_last = map(lambda c: (c, c ^ odd), range(n_axis))
+        small = lax.ppermute(block_now, axis_key, list(block_last))
+        all_rows = jnp.stack([block_now, small])
+        y = lax.axis_index(axis_key)
+        z1 = y >> u & 1
+        block_now = jnp.where(z1 == 0, all_rows, all_rows[::-1]).reshape(-1, *work_x.shape)
+    return block_now
 
 
 def modulate(values, weight_gain, offset, stretch):
@@ -158,7 +178,7 @@
     ).astype(jnp.float32)
     middle = values + shifts[2] * branch
     normed_two = modulate(middle, norm_two, shifts[3], shifts[4]).astype(jnp.bfloat16)
-    normed_two_all = lax.all_gather(normed_two, "tensor", axis=0, tiled=True)
+    normed_two_all = column_order(refer_the_pairs_all(normed_two, "tensor"), 0)
     hidden = jnp.dot(
         normed_two_all, up_full, preferred_element_type=jnp.float32
     ) + up_bias_full.astype(jnp.float32)

time: 1270 us -> 1230 us (0.969)
  waiting for transfers between devices: 596 us -> 547 us
    all_gather x1 -> x0, waiting for transfers between devices: 41.2 us -> none  [per_device(): normed_two_all = lax.all_gather(normed_two, 'tensor', axis=0, tiled=True)]
  transfers between devices with their start and end apart: 17 -> 17, of which waited for: 13 -> 10; matrix products, arithmetic and copies ran while one was open for 9% -> 10% of each run, Pallas kernels for 0% -> 0%
where the time goes in v1:
time: 1230 us
  waiting for transfers between devices  547 us (44%)
  matrix products  284 us (23%)
  blocking collectives  238 us (19%)
  other arithmetic  80.4 us (7%)
  local copies, waits for them, and re-layouts  59 us (5%)
  between operations  16.2 us (1%)
    unnamed x4, blocking collectives  148 us
    reduce_scatter x1, waiting for transfers between devices, per_device(): lax.psum_scatter(mod_weight_adj, ('dp', 'tensor'), scatter_dimension=2, t...  105 us
    reduce_scatter x1, waiting for transfers between devices, per_device(): lax.psum_scatter(inlet_adj, 'dp', scatter_dimension=0, tiled=True)  93.3 us
    reduce_scatter x1, waiting for transfers between devices, per_device(): lax.psum_scatter(down_adj, 'dp', scatter_dimension=0, tiled=True)  73.2 us
    all_gather x1, blocking collectives, per_device(): lax.all_gather(modulator_bias, ('dp', 'tensor'), axis=1, tiled=True)  67.5 us
    reduce_scatter x1, waiting for transfers between devices, per_device(): lax.psum_scatter(outlet_adj, 'dp', scatter_dimension=2, tiled=True)  66.6 us
    all_gather x1, waiting for transfers between devices, per_device(): mlp_slope_all = lax.all_gather(mlp_slope, 'tensor', axis=0, tiled=True)  40.8 us
    all_gather x1, waiting for transfers between devices, per_device(): lax.all_gather(branch_slope, 'tensor', axis=0, tiled=True)  38.1 us
  transfers between devices with their start and end apart: 17, of which 10 were waited for; matrix products, arithmetic and copies ran while one was open for 10% of the time, Pallas kernels for 0%

profile of v1, /device:TPU:0, one launch (start us, length us, event | category | flops | bytes accessed | tf_op | source)
XLA Modules:
  0.0 1227.4 jit_solution(3400326489492390829)
XLA Ops:
  11.3 42.2 %all-reduce.10 = (bf16[768]{0:T(1024)(128)(2,1)}, bf16[768]{0:T(1024)(128)(2,1)S(1)}, bf16[768]{0:T(1024)(128)(2,1)}) all-reduce(bf16[768]{0:T(1024)(128)(2,1)S(1)} %dynamic-update-slice.1, bf16[768]{0:T(1024)(128)(2,1)S(1)} %dynamic-update-slice, ...), channel_id=1, replica_groups=mesh['dp'=16,'tensor'=2] {'dp','tensor'}, use_global_device_ids=true, to_apply=%add.1 | all-reduce | flops 2304 | bytes 9216
  53.5 67.5 %all-gather = bf16[32,24,6]{1,2,0:T(8,128)(2,1)S(1)} all-gather(bf16[1,24,6]{1,2,0:T(8,128)(2,1)} %bitcast.214), channel_id=1, replica_groups=mesh['dp'=16,'tensor'=2] {'dp','tensor'}, dimensions={0}, use_global_device_ids=true | all-gather | bytes 9504 | tf_op jit(solution)/shard_map/all_gather | solution.py:137
  143.4 22.4 %all_gather.48 = bf16[6,64,768]{1,2,0:T(8,128)(2,1)} all-gather(bf16[6,64,48]{1,2,0:T(8,128)(2,1)S(1)} %copy-done.29), channel_id=1, replica_groups=mesh['dp'=16,'tensor'=2] {'dp'}, dimensions={2}, use_global_device_ids=true | all-gather | bytes 626688 | tf_op jit(solution)/shard_map/all_gather | solution.py:83
  194.5 59.2 %while.39 = (s32[]{:T(128)}, bf16[6,1792,64]{1,2,0:T(8,128)(2,1)}, f32[6,1792]{1,0:T(8,128)S(1)}, bf16[6,1792,64]{2,1,0:T(8,128)(2,1)}, bf16[6,1792,64]{2,1,0:T(...) while((s32[]{:T(128)}, bf16[6,1792,64]{1,2,0:T(8,128)(2,1)}, ...), condition=%wide.region_7.8_spmd, body=%wide.region_4.7_spmd.sunk | while | flops 847886592 | bytes 43440232 | solution.py:171
  261.1 34.8 %reduce-scatter.11.cloned.1.call-done = bf16[896,768]{1,0:T(8,128)(2,1)} async-done(((bf16[1792,768]{1,0:T(8,128)(2,1)}), bf16[896,768]{1,0:T(8,128)(2,1)}) %reduce-scatter.11.cloned.1.call-update) | async-done | bytes 1376272 | tf_op jit(solution)/shard_map/reduce_scatter | solution.py:176
  305.1 33.6 %all-reduce.2 = bf16[1536]{0:T(1024)(128)(2,1)S(1)} all-reduce(bf16[1536]{0:T(1024)(128)(2,1)S(1)} %dynamic-update-slice.2), channel_id=1, replica_groups=mesh['dp'=16,'tensor'=2] {'dp'}, use_global_device_ids=true, to_apply=%add.2 | all-reduce | flops 1536 | bytes 6144
  342.8 12.3 %multiply_convert_fusion.1 = (bf16[1792,1536]{1,0:T(8,128)(2,1)}, f32[1792,1536]{1,0:T(8,128)}) fusion(f32[1536]{0:T(1024)S(1)} %convert_element_type.125, bf16[1792,768]{1,0:T(8,128)(2,1)} %bitcast.208, bf16[768,1536]{0,1:T(8,128)(2,1)} %all-gather.15.cloned.1.call-done), kind=kOutput, calls=%fused_computation.64 | convolution fusion | flops 4255383552 | bytes 21633024 | tf_op jit(solution)/shard_map/dot_general | solution.py:182
  355.2 28.3 %all-gather.17.cloned.1.call-done = bf16[1536,768]{1,0:T(8,128)(2,1)} async-done(((bf16[96,768]{1,0:T(8,128)(2,1)}), bf16[1536,768]{1,0:T(8,128)(2,1)}) %all-gather.17.cloned.1.call-update) | async-done | bytes 2359312 | tf_op jit(solution)/shard_map/all_gather | solution.py:85
  383.5 40.8 %all-gather.19.cloned.1.call-done = bf16[1792,768]{1,0:T(8,128)(2,1)} async-done(((bf16[896,768]{1,0:T(8,128)(2,1)}), bf16[1792,768]{1,0:T(8,128)(2,1)}) %all-gather.19.cloned.1.call-update) | async-done | bytes 2752528 | tf_op jit(solution)/shard_map/all_gather | solution.py:200
  424.3 15.4 %convert_reduce_fusion = (f32[1536]{0:T(1024)}, bf16[1792,1536]{1,0:T(8,128)(2,1)S(1)}) fusion(f32[1792,1536]{1,0:T(8,128)} %get-tuple-element.309, f32[1536]{0:T(1024)S(1)} %convert_element_type.125, bf16[1792,768]{1,0:T(8,128)(2,1)} %all-gather.19.cloned.1.call-done, bf16[1536,768]{1,0:T(8,128)(2,1)} %all-gather.17.cloned.1.call-done), kind=kOutput, calls=%fused_computation.63 | convolution fusion | flops 4291164672 | bytes 21639168 | tf_op jit(solution)/shard_map/dot_general | solution.py:202
  447.9 9.3 convolution_convert_fusion.1
  457.9 29.1 %reduce-scatter.15.cloned.1.call-done = bf16[896,768]{1,0:T(8,128)(2,1)} async-done(((bf16[1792,768]{1,0:T(8,128)(2,1)}), bf16[896,768]{1,0:T(8,128)(2,1)}) %reduce-scatter.15.cloned.1.call-update) | async-done | bytes 1376272 | tf_op jit(solution)/shard_map/reduce_scatter | solution.py:208
  493.1 35.3 %reduce-scatter.13.cloned.1.call-done = bf16[896,768]{1,0:T(8,128)(2,1)} async-done(((bf16[1792,768]{1,0:T(8,128)(2,1)}), bf16[896,768]{1,0:T(8,128)(2,1)}) %reduce-scatter.13.cloned.1.call-update) | async-done | bytes 1376272 | tf_op jit(solution)/shard_map/reduce_scatter | solution.py:187
  539.9 38.1 %all-gather.21.cloned.1.call-done = bf16[1792,768]{1,0:T(8,128)(2,1)} async-done(((bf16[896,768]{1,0:T(8,128)(2,1)}), bf16[1792,768]{1,0:T(8,128)(2,1)}) %all-gather.21.cloned.1.call-update) | async-done | bytes 2752528 | tf_op jit(solution)/shard_map/all_gather | solution.py:216
  586.2 154.8 %while.40 = (s32[]{:T(128)}, f32[6,1792,64]{1,2,0:T(8,128)}, f32[6,1792,64]{1,2,0:T(8,128)}, bf16[6,1792,64]{1,2,0:T(8,128)(2,1)}, bf16[6,1792,64]{2,1,0:T(8,128...) while((s32[]{:T(128)}, f32[6,1792,64]{1,2,0:T(8,128)}, ...), condition=%wide.region_17.18_spmd, body=%wide.region_15.17_spmd.sunk | while | flops 2087319808 | bytes 155558096 | solution.py:222
  758.2 9.3 fusion.116
  769.2 9.2 fusion.117
  785.0 10.3 fusion.55
  803.4 34.1 %all-reduce.6 = f32[1536]{0:T(1024)S(1)} all-reduce(f32[1536]{0:T(1024)S(1)} %copy-done.44), channel_id=11, replica_groups=mesh['dp'=16,'tensor'=2] {'dp'}, use_global_device_ids=true, to_apply=%region_29.30.clone | all-reduce | flops 1536 | bytes 12288
  838.1 38.4 %all-reduce.9 = (f32[768]{0:T(1024)S(1)}, f32[768]{0:T(1024)S(1)}, f32[768]{0:T(1024)S(1)}, f32[6,768]{1,0:T(8,128)S(1)}) all-reduce(f32[768]{0:T(1024)S(1)} %get-tuple-element.216, f32[768]{0:T(1024)S(1)} %copy-done.39, f32[768]{0:T(1024)S(1)} %mul.488, ...), channel_id=6, replica_groups=mesh['dp'=16,'tensor'=2] {'dp','tensor'}, use_global_device_ids=true, to_apply=%region_22.23.clone | all-reduce | flops 6912 | bytes 55296
  882.4 73.2 %reduce-scatter.25.cloned.1.call-done = f32[96,768]{1,0:T(8,128)} async-done(((f32[1536,768]{1,0:T(8,128)}), f32[96,768]{1,0:T(8,128)}) %reduce-scatter.25.cloned.1.call-update) | async-done | bytes 294928 | tf_op jit(solution)/shard_map/reduce_scatter | solution.py:252
  955.7 66.6 %reduce-scatter.21.cloned.1.call-done = f32[6,64,48]{1,2,0:T(8,128)} async-done(((f32[6,64,768]{1,2,0:T(8,128)}), f32[6,64,48]{1,2,0:T(8,128)}) %reduce-scatter.21.cloned.1.call-update) | async-done | bytes 73744 | tf_op jit(solution)/shard_map/reduce_scatter | solution.py:250
  1022.3 93.3 %reduce-scatter.19.cloned.1.call-done = f32[48,3,6,64]{3,0,2,1:T(8,128)} async-done(((f32[768,3,6,64]{3,0,2,1:T(8,128)}), f32[48,3,6,64]{3,0,2,1:T(8,128)}) %reduce-scatter.19.cloned.1.call-update) | async-done | bytes 221200 | tf_op jit(solution)/shard_map/reduce_scatter | solution.py:249
  1115.6 105.1 %reduce-scatter.27.cloned.1.call-done = f32[128,6,24]{0,2,1:T(8,128)} async-done(((f32[128,6,768]{0,2,1:T(8,128)}), f32[128,6,24]{0,2,1:T(8,128)}) %reduce-scatter.27.cloned.1.call-update) | async-done | bytes 73744 | tf_op jit(solution)/shard_map/reduce_scatter | solution.py:260
  (381 shorter events, 365.1 us)
Async XLA Ops:
  7.2 115.7 %copy-start.3 = (bf16[896,768]{1,0:T(8,128)(2,1)S(1)}, bf16[896,768]{1,0:T(8,128)(2,1)}, u32[]{:S(2)}) copy-start(bf16[896,768]{1,0:T(8,128)(2,1)} %param.21) | copy-start | bytes 4128772
  7.2 116.3 %copy-start.48 = (f32[1,128]{1,0:T(1,128)S(1)}, f32[1,128]{1,0:T(1,128)}, u32[]{:S(2)}) copy-start(f32[1,128]{1,0:T(1,128)} %param.23) | copy-start | bytes 1540
  7.2 116.3 %all-gather.9.cloned.1.call-start = ((), (), s32[]{:S(2)}) async-start(), calls=%async_computation.9 | async-start | bytes 1216512 | tf_op jit(solution)/shard_map/all_gather | solution.py:138
  7.9 159.5 %all-gather.13.cloned.1.call-start = ((), (), s32[]{:S(2)}) async-start(), calls=%async_computation.11 | async-start | bytes 3760128 | tf_op jit(solution)/shard_map/all_gather | solution.py:82
  8.7 163.6 %all-gather.11.cloned.1.call-start = ((), (), s32[]{:S(2)}) async-start(), calls=%async_computation.10 | async-start | bytes 4128768 | tf_op jit(solution)/shard_map/all_gather | solution.py:160
  53.4 74.8 %copy-start.24 = (f32[768]{0:T(1024)}, f32[768]{0:T(1024)S(1)}, u32[]{:S(2)}) copy-start(f32[768]{0:T(1024)S(1)} %convert_element_type.115) | copy-start | bytes 9220
  128.3 167.6 %reduce-scatter.11.cloned.1.call-start = ((), (), s32[]{:S(2)}) async-start(), calls=%async_computation.12 | async-start | bytes 4128768 | tf_op jit(solution)/shard_map/reduce_scatter | solution.py:176
  259.4 36.4 %copy-start.21 = (f32[768]{0:T(1024)S(1)}, f32[768]{0:T(1024)}, u32[]{:S(2)}) copy-start(f32[768]{0:T(1024)} %get-tuple-element.226) | copy-start | bytes 9220
  259.4 83.4 %all-gather.15.cloned.1.call-start = ((), (), s32[]{:S(2)}) async-start(), calls=%async_computation.13 | async-start | bytes 2506752 | tf_op jit(solution)/shard_map/all_gather | solution.py:84
  260.0 123.5 %all-gather.17.cloned.1.call-start = ((), (), s32[]{:S(2)}) async-start(), calls=%async_computation.14 | async-start | bytes 2506752 | tf_op jit(solution)/shard_map/all_gather | solution.py:85
  260.6 163.7 %all-gather.19.cloned.1.call-start = ((), (), s32[]{:S(2)}) async-start(), calls=%async_computation.16 | async-start | bytes 4128768 | tf_op jit(solution)/shard_map/all_gather | solution.py:200
  301.7 37.0 %collective-permute-start = (bf16[1,896,768]{2,1,0:T(8,128)(2,1)}, bf16[1,896,768]{2,1,0:T(8,128)(2,1)}, u32[]{:S(2)}, u32[]{:S(2)}) collective-permute-start(bf16[1,896,768]{2,1,0:T(8,128)(2,1)} %get-tuple-element.295), channel_id=1, source_target_pairs={{0,1},{1,0},{2,3},{3,2},{4,5},{5,4},{6,7},{7,6},{8,9},{9,8},{10,11... | collective-permute-start | bytes 4128776 | tf_op jit(solution)/shard_map/ppermute | solution.py:25
  303.5 183.5 %reduce-scatter.15.cloned.1.call-start = ((), (), s32[]{:S(2)}) async-start(), calls=%async_computation.17 | async-start | bytes 4128768 | tf_op jit(solution)/shard_map/reduce_scatter | solution.py:208
  447.7 80.7 %reduce-scatter.13.cloned.1.call-start = ((), (), s32[]{:S(2)}) async-start(), calls=%async_computation.15 | async-start | bytes 4128768 | tf_op jit(solution)/shard_map/reduce_scatter | solution.py:187
  457.2 120.8 %all-gather.21.cloned.1.call-start = ((), (), s32[]{:S(2)}) async-start(), calls=%async_computation.18 | async-start | bytes 4128768 | tf_op jit(solution)/shard_map/all_gather | solution.py:216
  537.4 258.6 %reduce-scatter.17.cloned.1.call-start = ((), (), s32[]{:S(2)}) async-start(), calls=%async_computation.19 | async-start | bytes 4128768 | tf_op jit(solution)/shard_map/reduce_scatter | solution.py:237
  756.4 126.0 %reduce-scatter.23.cloned.1.call-start = ((), (), s32[]{:S(2)}) async-start(), calls=%async_computation.22 | async-start | bytes 5013504 | tf_op jit(solution)/shard_map/reduce_scatter | solution.py:251
  767.5 188.2 %reduce-scatter.25.cloned.1.call-start = ((), (), s32[]{:S(2)}) async-start(), calls=%async_computation.23 | async-start | bytes 5013504 | tf_op jit(solution)/shard_map/reduce_scatter | solution.py:252
  778.5 243.8 %reduce-scatter.21.cloned.1.call-start = ((), (), s32[]{:S(2)}) async-start(), calls=%async_computation.21 | async-start | bytes 2506752 | tf_op jit(solution)/shard_map/reduce_scatter | solution.py:250
  784.9 330.7 %reduce-scatter.19.cloned.1.call-start = ((), (), s32[]{:S(2)}) async-start(), calls=%async_computation.20 | async-start | bytes 7520256 | tf_op jit(solution)/shard_map/reduce_scatter | solution.py:249
  795.4 425.2 %reduce-scatter.27.cloned.1.call-start = ((), (), s32[]{:S(2)}) async-start(), calls=%async_computation.24 | async-start | bytes 2433024 | tf_op jit(solution)/shard_map/reduce_scatter | solution.py:260
  800.8 37.3 %copy-start.31 = (f32[768]{0:T(1024)S(1)}, f32[768]{0:T(1024)}, u32[]{:S(2)}) copy-start(f32[768]{0:T(1024)} %get-tuple-element.221) | copy-start | bytes 9220
  800.8 37.3 %copy-start.36 = (f32[768]{0:T(1024)S(1)}, f32[768]{0:T(1024)}, u32[]{:S(2)}) copy-start(f32[768]{0:T(1024)} %get-tuple-element.297) | copy-start | bytes 9220
  800.8 37.3 %copy-start.39 = (f32[768]{0:T(1024)S(1)}, f32[768]{0:T(1024)}, u32[]{:S(2)}) copy-start(f32[768]{0:T(1024)} %get-tuple-element.213) | copy-start | bytes 9220
  (64 other events, 207.2 us)
Sparse Core Ops, SparseCore 0:
  10.9 54.4 all-gather.8
  67.6 47.3 all-gather.12
  128.4 36.3 all-gather.10
  259.6 36.2 reduce-scatter.10
  298.0 42.2 all-gather.14
  342.4 41.0 all-gather.16
  385.0 39.1 all-gather.18
  447.8 39.0 reduce-scatter.14
  489.2 39.0 reduce-scatter.12
  537.6 40.4 all-gather.20
  756.5 39.0 reduce-scatter.16
  800.0 76.4 reduce-scatter.22
  880.9 74.7 reduce-scatter.24
  959.9 62.4 reduce-scatter.20
  1026.7 88.8 reduce-scatter.18
  1121.3 99.2 reduce-scatter.26
